TPU v7x, 32 devices: a whole 2x2x4 slice. The times are simulated.
32 devices in a mesh: region: 8 (over y, x, core), cuts: 4 (over z).
Axes of the slice: x: 2, y: 2, z: 4, core: 2. Of those that a mesh axis runs over, the one named last changes fastest.
Arguments:
- history: bfloat16 [8, 8192, 128], P(None, ('region', 'cuts')), may hold values from -6 to 6
- incident: bfloat16 [4, 8192, 128], P(None, ('region', 'cuts')), may hold values from -6 to 6
- self_inverse: bfloat16 [8192, 256], P(('region', 'cuts')), may hold values from -0.375 to 0.375
- lag_kernels: bfloat16 [384, 8, 256, 256], P(('region', 'cuts')), may hold values from -0.02734375 to 0.02734375
- pair_partner: int32 [384], P(('region', 'cuts')), may hold values from 0 to 11
- pair_lags: int32 [384], P(('region', 'cuts')), may hold values from 1 to 8
Outputs:
- densities: bfloat16 [4, 8192, 128], P(None, ('region', 'cuts'))
Inputs may be any that keep to these rules, and one draw needn't show every extreme that they name: `pair_partner`: codes below 4 name a block of the region before the owner's, codes from 8 on one of the region after it, the others one of the owner's region; the same block may be named by several pairs, and a pair's partner may be its owner. Pair p uses lag matrices 1 to pair_lags[p]; the rest are stored but unused.
All inputs are finite; a program needn't handle non-finite values.
Results may differ from a plain program's by a relative error of at most 0.0095.
Values may be sent and summed in bfloat16 or wider, within the bound.
No kernel may reach another device: no remote copies, remote signals or barrier semaphores. Data moves between devices by JAX's collectives and lax.ppermute only.
A program may use at most 128 MiB of HBM per device.

v0:
```python
import jax
import jax.numpy as jnp
from jax import lax
from jax.sharding import PartitionSpec as P


def padded(block, sides, width):
    for axis, dim in sides:
        count = lax.axis_size(axis)
        forward = [(i, i + 1) for i in range(count - 1)]
        forward.append((count - 1, 0))
        backward = [(target, source) for source, target in forward]
        low = lax.ppermute(
            lax.slice_in_dim(block, block.shape[dim] - width, None, axis=dim), axis, forward
        )
        high = lax.ppermute(lax.slice_in_dim(block, 0, width, axis=dim), axis, backward)
        block = jnp.concatenate([low, block, high], axis=dim)
    return block


def shifted(block, axis, distance):
    devices = range(lax.axis_size(axis))
    route = [((i - distance) % len(devices), i) for i in devices]
    return lax.ppermute(block, axis, route)


def lag_gate(pair_lags, lag_total):
    lag_ids = lax.iota(jnp.int32, lag_total) + 1
    return (lag_ids[None, :] <= pair_lags[:, None]).astype(jnp.bfloat16)


def near_field(lag_kernels, window, recent, pair_partner, gate_table, cut_count, own_cut):
    partner_hist = jnp.take(window, pair_partner, axis=1)
    partner_hist = partner_hist * jnp.transpose(gate_table)[:, :, None, None]
    forward = jnp.einsum(
        "plij,lpjr->ir", lag_kernels, partner_hist, preferred_element_type=jnp.float32
    )
    own_hist = gate_table[:, :, None, None] * recent[None]
    backward = jnp.einsum(
        "plij,plir->pjr", lag_kernels, own_hist, preferred_element_type=jnp.float32
    )
    slot_codes = lax.iota(jnp.int32, 3 * cut_count)
    select = (slot_codes[:, None] == pair_partner[None, :]).astype(jnp.float32)
    spread = jnp.einsum("qp,pjr->qjr", select, backward, precision=lax.Precision.HIGHEST)
    own_slot = (slot_codes == cut_count + own_cut).astype(jnp.float32)
    return spread + own_slot[:, None, None] * forward[None]


def on_device(history, incident, self_inverse, lag_kernels, pair_partner, pair_lags):
    lag_total = history.shape[0]
    step_total = incident.shape[0]
    panel_count = history.shape[1]
    column_count = history.shape[2]
    cut_count = lax.axis_size("cuts")
    own_cut = lax.axis_index("cuts")
    gate_table = lag_gate(pair_lags, lag_total)
    recent = history
    window = history
    outputs = []
    for step_now in range(step_total):
        stacked = lax.all_gather(recent[:, None, None], "cuts", axis=2, tiled=True)
        bordered = padded(stacked, (("region", 1),), 1)
        window = bordered.reshape(lag_total, 3 * cut_count, panel_count, column_count)
        partial_field = near_field(
            lag_kernels, window, recent, pair_partner, gate_table, cut_count, own_cut
        )
        grouped = partial_field.reshape(3, cut_count, panel_count, column_count)
        from_above = shifted(grouped[0].astype(jnp.bfloat16), "region", -1).astype(jnp.float32)
        from_below = shifted(grouped[2].astype(jnp.bfloat16), "region", 1).astype(jnp.float32)
        field_sum = lax.psum_scatter(
            grouped[1] + from_above + from_below, "cuts", scatter_dimension=0, tiled=True
        )[0]
        excess = (incident[step_now].astype(jnp.float32) - field_sum).astype(jnp.bfloat16)
        density = jnp.dot(self_inverse, excess, preferred_element_type=jnp.float32).astype(
            jnp.bfloat16
        )
        outputs.append(density)
        recent = jnp.concatenate([density[None], recent[:-1]], axis=0)
    return jnp.stack(outputs)


def solution(mesh):
    return jax.shard_map(
        on_device,
        mesh=mesh,
        in_specs=(
            P(None, ("region", "cuts"), None),
            P(None, ("region", "cuts"), None),
            P(("region", "cuts"), None),
            P(("region", "cuts"), None, None, None),
            P(("region", "cuts")),
            P(("region", "cuts")),
        ),
        out_specs=P(None, ("region", "cuts"), None),
        check_vma=False,
    )
```

profile of v0, /device:TPU:0, one launch (start us, length us, event | category | flops | bytes accessed | tf_op | source)
XLA Modules:
  0.0 628.3 jit_solution(11969034751456141057)
XLA Ops:
  7.3 1.2 copy.43
  9.3 48.0 %all-gather.9.cloned.1.call-done = bf16[8,1024,128]{2,1,0:T(8,128)(2,1)} async-done(((bf16[8,256,128]{2,1,0:T(8,128)(2,1)}), bf16[8,1024,128]{2,1,0:T(8,128)(2,1)}) %all-gather.9.cloned.1.call-update) | async-done | bytes 2097168 | tf_op jit(solution)/shard_map/all_gather | solution.py:61
  57.3 1.7 collective-permute-start.1
  59.0 7.6 %fusion.28 = f32[12,256,128]{1,2,0:T(8,128)} fusion(bf16[12,8,256,256]{3,2,1,0:T(8,128)(2,1)} %param.11, bf16[8,256,128]{1,2,0:T(8,128)(2,1)S(1)} %copy.43, bf16[12,8]{1,0:T(8,128)(2,1)S(1)} %compare_convert_fusion.1), kind=kOutput, calls=%fused_computation.44 | convolution fusion | flops 1613758464 | bytes 14680256 | tf_op jit(solution)/shard_map/plij,plir->pjr/dot_general | solution.py:39
  66.6 2.1 copy.44
  68.9 35.7 %collective-permute-done.1 = bf16[8,1,4,256,128]{4,3,2,1,0:T(8,128)(2,1)} collective-permute-done((bf16[8,1,4,256,128]{4,3,2,1,0:T(8,128)(2,1)}, bf16[8,1,4,256,128]{4,3,2,1,0:T(8,128)(2,1)}, u32[]{:S(2)}, u32[]{:S(2)}) %collective-permute-start.1) | collective-permute-done | bytes 2097184 | tf_op jit(solution)/shard_map/ppermute | solution.py:16
  104.6 1.9 collective-permute-done
  106.5 6.5 %pad_maximum_fusion = bf16[8,3,4,256,128]{4,3,2,1,0:T(8,128)(2,1)} fusion(bf16[8,1,4,256,128]{4,3,2,1,0:T(8,128)(2,1)} %collective-permute-done.1, bf16[8,1,4,256,128]{4,3,2,1,0:T(8,128)(2,1)} %bitcast.128, bf16[8,1,4,256,128]{4,3,2,1,0:T(8,128)(2,1)} %collective-permute-done), kind=kLoop, calls=%fused_computation.12 | loop fusion | flops 6291456 | bytes 12582912 | tf_op jit(solution)/shard_map/concatenate | solution.py:17
  113.0 6.9 %gather_fusion = bf16[12,8,256,128]{3,2,1,0:T(8,128)(2,1)} fusion(bf16[8,12,256,128]{3,2,1,0:T(8,128)(2,1)} %bitcast.123, s32[1024]{0:T(1024)S(1)} %pad_clamp_fusion), kind=kCustom, calls=%fused_computation.clone | custom fusion | bytes 12582960 | tf_op jit(solution)/shard_map/jit(_take)/gather | solution.py:33
  119.9 12.1 %fusion.40 = f32[256,128]{0,1:T(8,128)S(1)} fusion(bf16[12,8,256,256]{3,2,1,0:T(8,128)(2,1)} %param.11, bf16[12,8,256,128]{3,2,1,0:T(8,128)(2,1)} %gather_fusion, pred[12]{0:T(512)(128)(4,1)S(1)} %compare_and_fusion, bf16[8,12]{0,1:T(8,128)(2,1)S(1)} %compare_convert_fusion), kind=kOutput, calls=%fused_computation.48 | convolution fusion | flops 1616904192 | bytes 19005644 | tf_op jit(solution)/shard_map/plij,lpjr->ir/dot_general | solution.py:35
  132.1 1.3 fusion.95
  133.7 2.6 collective-permute-start.2
  136.3 6.1 collective-permute-done.3
  143.6 19.7 %reduce-scatter.5.cloned.1.call-done = f32[1,256,128]{2,1,0:T(8,128)} async-done(((f32[4,256,128]{2,1,0:T(8,128)}), f32[1,256,128]{2,1,0:T(8,128)}) %reduce-scatter.5.cloned.1.call-update) | async-done | bytes 131088 | tf_op jit(solution)/shard_map/reduce_scatter | solution.py:70
  163.4 1.1 fusion.60
  164.6 0.9 pad_maximum_fusion.4
  165.5 44.0 %all-gather.11.cloned.1.call-done = bf16[8,1024,128]{2,1,0:T(8,128)(2,1)} async-done(((bf16[8,256,128]{2,1,0:T(8,128)(2,1)}), bf16[8,1024,128]{2,1,0:T(8,128)(2,1)}) %all-gather.11.cloned.1.call-update) | async-done | bytes 2097168 | tf_op jit(solution)/shard_map/all_gather | solution.py:61
  209.5 1.7 collective-permute-start.5
  211.6 1.2 copy.50
  212.9 7.6 %fusion.31 = f32[12,256,128]{1,2,0:T(8,128)} fusion(bf16[12,8,256,256]{3,2,1,0:T(8,128)(2,1)} %param.11, bf16[8,256,128]{1,2,0:T(8,128)(2,1)S(1)} %copy.50, bf16[12,8]{1,0:T(8,128)(2,1)S(1)} %compare_convert_fusion.1), kind=kOutput, calls=%fused_computation.45 | convolution fusion | flops 1613758464 | bytes 14680256 | tf_op jit(solution)/shard_map/plij,plir->pjr/dot_general | solution.py:39
  220.5 2.1 copy.51
  222.6 34.6 %collective-permute-done.5 = bf16[8,1,4,256,128]{4,3,2,1,0:T(8,128)(2,1)} collective-permute-done((bf16[8,1,4,256,128]{4,3,2,1,0:T(8,128)(2,1)}, bf16[8,1,4,256,128]{4,3,2,1,0:T(8,128)(2,1)}, u32[]{:S(2)}, u32[]{:S(2)}) %collective-permute-start.5) | collective-permute-done | bytes 2097184 | tf_op jit(solution)/shard_map/ppermute | solution.py:16
  257.2 1.5 collective-permute-done.4
  258.7 6.5 %pad_maximum_fusion.1 = bf16[8,3,4,256,128]{4,3,2,1,0:T(8,128)(2,1)} fusion(bf16[8,1,4,256,128]{4,3,2,1,0:T(8,128)(2,1)} %collective-permute-done.5, bf16[8,1,4,256,128]{4,3,2,1,0:T(8,128)(2,1)} %bitcast.134, bf16[8,1,4,256,128]{4,3,2,1,0:T(8,128)(2,1)} %collective-permute-done.4), kind=kLoop, calls=%fused_computation.13 | loop fusion | flops 6291456 | bytes 12582912 | tf_op jit(solution)/shard_map/concatenate | solution.py:17
  265.1 6.9 %gather_fusion.1 = bf16[12,8,256,128]{3,2,1,0:T(8,128)(2,1)} fusion(bf16[8,12,256,128]{3,2,1,0:T(8,128)(2,1)} %bitcast.124, s32[1024]{0:T(1024)S(1)} %pad_clamp_fusion), kind=kCustom, calls=%fused_computation.1.clone | custom fusion | bytes 12582960 | tf_op jit(solution)/shard_map/jit(_take)/gather | solution.py:33
  272.1 12.1 %fusion.45 = f32[256,128]{0,1:T(8,128)S(1)} fusion(bf16[12,8,256,256]{3,2,1,0:T(8,128)(2,1)} %param.11, bf16[12,8,256,128]{3,2,1,0:T(8,128)(2,1)} %gather_fusion.1, pred[12]{0:T(512)(128)(4,1)S(1)} %copy-done.9, bf16[8,12]{0,1:T(8,128)(2,1)S(1)} %copy-done.5), kind=kOutput, calls=%fused_computation.49 | convolution fusion | flops 1616904192 | bytes 19005644 | tf_op jit(solution)/shard_map/plij,lpjr->ir/dot_general | solution.py:35
  284.3 1.3 fusion.96
  285.8 2.6 collective-permute-start.6
  288.5 6.1 collective-permute-done.7
  295.8 19.6 %reduce-scatter.7.cloned.1.call-done = f32[1,256,128]{2,1,0:T(8,128)} async-done(((f32[4,256,128]{2,1,0:T(8,128)}), f32[1,256,128]{2,1,0:T(8,128)}) %reduce-scatter.7.cloned.1.call-update) | async-done | bytes 131088 | tf_op jit(solution)/shard_map/reduce_scatter | solution.py:70
  315.4 1.1 fusion.61
  316.7 0.9 pad_maximum_fusion.5
  317.6 44.0 %all-gather.13.cloned.1.call-done = bf16[8,1024,128]{2,1,0:T(8,128)(2,1)} async-done(((bf16[8,256,128]{2,1,0:T(8,128)(2,1)}), bf16[8,1024,128]{2,1,0:T(8,128)(2,1)}) %all-gather.13.cloned.1.call-update) | async-done | bytes 2097168 | tf_op jit(solution)/shard_map/all_gather | solution.py:61
  361.6 1.7 collective-permute-start.9
  363.4 1.2 copy.57
  364.7 7.6 %fusion.34 = f32[12,256,128]{1,2,0:T(8,128)} fusion(bf16[12,8,256,256]{3,2,1,0:T(8,128)(2,1)} %param.11, bf16[8,256,128]{1,2,0:T(8,128)(2,1)S(1)} %copy.57, bf16[12,8]{1,0:T(8,128)(2,1)S(1)} %compare_convert_fusion.1), kind=kOutput, calls=%fused_computation.46 | convolution fusion | flops 1613758464 | bytes 14680256 | tf_op jit(solution)/shard_map/plij,plir->pjr/dot_general | solution.py:39
  372.3 2.1 copy.58
  374.5 34.6 %collective-permute-done.9 = bf16[8,1,4,256,128]{4,3,2,1,0:T(8,128)(2,1)} collective-permute-done((bf16[8,1,4,256,128]{4,3,2,1,0:T(8,128)(2,1)}, bf16[8,1,4,256,128]{4,3,2,1,0:T(8,128)(2,1)}, u32[]{:S(2)}, u32[]{:S(2)}) %collective-permute-start.9) | collective-permute-done | bytes 2097184 | tf_op jit(solution)/shard_map/ppermute | solution.py:16
  409.0 1.8 collective-permute-done.8
  410.8 6.5 %pad_maximum_fusion.2 = bf16[8,3,4,256,128]{4,3,2,1,0:T(8,128)(2,1)} fusion(bf16[8,1,4,256,128]{4,3,2,1,0:T(8,128)(2,1)} %collective-permute-done.9, bf16[8,1,4,256,128]{4,3,2,1,0:T(8,128)(2,1)} %bitcast.137, bf16[8,1,4,256,128]{4,3,2,1,0:T(8,128)(2,1)} %collective-permute-done.8), kind=kLoop, calls=%fused_computation.14 | loop fusion | flops 6291456 | bytes 12582912 | tf_op jit(solution)/shard_map/concatenate | solution.py:17
  417.3 6.9 %gather_fusion.2 = bf16[12,8,256,128]{3,2,1,0:T(8,128)(2,1)} fusion(bf16[8,12,256,128]{3,2,1,0:T(8,128)(2,1)} %bitcast.125, s32[1024]{0:T(1024)S(1)} %pad_clamp_fusion), kind=kCustom, calls=%fused_computation.2.clone | custom fusion | bytes 12582960 | tf_op jit(solution)/shard_map/jit(_take)/gather | solution.py:33
  424.2 12.1 %fusion.50 = f32[256,128]{0,1:T(8,128)S(1)} fusion(bf16[12,8,256,256]{3,2,1,0:T(8,128)(2,1)} %param.11, bf16[12,8,256,128]{3,2,1,0:T(8,128)(2,1)} %gather_fusion.2, pred[12]{0:T(512)(128)(4,1)S(1)} %copy-done.10, bf16[8,12]{0,1:T(8,128)(2,1)S(1)} %copy-done.6), kind=kOutput, calls=%fused_computation.50 | convolution fusion | flops 1616904192 | bytes 19005644 | tf_op jit(solution)/shard_map/plij,lpjr->ir/dot_general | solution.py:35
  436.4 1.3 fusion.97
  438.0 2.6 collective-permute-start.10
  440.6 6.1 collective-permute-done.11
  447.9 19.5 %reduce-scatter.9.cloned.1.call-done = f32[1,256,128]{2,1,0:T(8,128)} async-done(((f32[4,256,128]{2,1,0:T(8,128)}), f32[1,256,128]{2,1,0:T(8,128)}) %reduce-scatter.9.cloned.1.call-update) | async-done | bytes 131088 | tf_op jit(solution)/shard_map/reduce_scatter | solution.py:70
  467.4 1.1 fusion.62
  468.7 0.9 pad_maximum_fusion.6
  469.6 44.0 %all-gather.15.cloned.1.call-done = bf16[8,1024,128]{2,1,0:T(8,128)(2,1)} async-done(((bf16[8,256,128]{2,1,0:T(8,128)(2,1)}), bf16[8,1024,128]{2,1,0:T(8,128)(2,1)}) %all-gather.15.cloned.1.call-update) | async-done | bytes 2097168 | tf_op jit(solution)/shard_map/all_gather | solution.py:61
  513.6 1.7 collective-permute-start.13
  515.4 1.2 copy.64
  516.7 7.6 %fusion.37 = f32[12,256,128]{1,2,0:T(8,128)} fusion(bf16[12,8,256,256]{3,2,1,0:T(8,128)(2,1)} %param.11, bf16[8,256,128]{1,2,0:T(8,128)(2,1)S(1)} %copy.64, bf16[12,8]{1,0:T(8,128)(2,1)S(1)} %compare_convert_fusion.1), kind=kOutput, calls=%fused_computation.47 | convolution fusion | flops 1613758464 | bytes 14680256 | tf_op jit(solution)/shard_map/plij,plir->pjr/dot_general | solution.py:39
  524.3 2.1 copy.65
  526.4 34.6 %collective-permute-done.13 = bf16[8,1,4,256,128]{4,3,2,1,0:T(8,128)(2,1)} collective-permute-done((bf16[8,1,4,256,128]{4,3,2,1,0:T(8,128)(2,1)}, bf16[8,1,4,256,128]{4,3,2,1,0:T(8,128)(2,1)}, u32[]{:S(2)}, u32[]{:S(2)}) %collective-permute-start.13) | collective-permute-done | bytes 2097184 | tf_op jit(solution)/shard_map/ppermute | solution.py:16
  561.0 1.7 collective-permute-done.12
  562.7 6.5 %pad_maximum_fusion.3 = bf16[8,3,4,256,128]{4,3,2,1,0:T(8,128)(2,1)} fusion(bf16[8,1,4,256,128]{4,3,2,1,0:T(8,128)(2,1)} %collective-permute-done.13, bf16[8,1,4,256,128]{4,3,2,1,0:T(8,128)(2,1)} %bitcast.131, bf16[8,1,4,256,128]{4,3,2,1,0:T(8,128)(2,1)} %collective-permute-done.12), kind=kLoop, calls=%fused_computation.15 | loop fusion | flops 6291456 | bytes 12582912 | tf_op jit(solution)/shard_map/concatenate | solution.py:17
  569.2 6.9 %gather_fusion.3 = bf16[12,8,256,128]{3,2,1,0:T(8,128)(2,1)} fusion(bf16[8,12,256,128]{3,2,1,0:T(8,128)(2,1)} %bitcast.122, s32[1024]{0:T(1024)S(1)} %pad_clamp_fusion), kind=kCustom, calls=%fused_computation.3.clone | custom fusion | bytes 12582960 | tf_op jit(solution)/shard_map/jit(_take)/gather | solution.py:33
  576.1 12.1 %fusion.55 = f32[256,128]{0,1:T(8,128)S(1)} fusion(bf16[12,8,256,256]{3,2,1,0:T(8,128)(2,1)} %param.11, bf16[12,8,256,128]{3,2,1,0:T(8,128)(2,1)} %gather_fusion.3, pred[12]{0:T(512)(128)(4,1)S(1)} %copy-done.10, bf16[8,12]{0,1:T(8,128)(2,1)S(1)} %copy-done.6), kind=kOutput, calls=%fused_computation.51 | convolution fusion | flops 1616904192 | bytes 19005644 | tf_op jit(solution)/shard_map/plij,lpjr->ir/dot_general | solution.py:35
  588.3 1.3 fusion.98
  589.9 2.6 collective-permute-start.14
  592.5 6.1 collective-permute-done.15
  599.7 19.5 %reduce-scatter.11.cloned.1.call-done = f32[1,256,128]{2,1,0:T(8,128)} async-done(((f32[4,256,128]{2,1,0:T(8,128)}), f32[1,256,128]{2,1,0:T(8,128)}) %reduce-scatter.11.cloned.1.call-update) | async-done | bytes 131088 | tf_op jit(solution)/shard_map/reduce_scatter | solution.py:70
  619.2 1.1 fusion.63
  620.4 0.8 copy.70
  (80 shorter events, 8.7 us)
Async XLA Ops:
  6.5 156.8 %copy-start = (bf16[256,256]{1,0:T(8,128)(2,1)S(1)}, bf16[256,256]{1,0:T(8,128)(2,1)}, u32[]{:S(2)}) copy-start(bf16[256,256]{1,0:T(8,128)(2,1)} %param.10) | copy-start | bytes 393220
  6.5 50.8 %all-gather.9.cloned.1.call-start = ((), (), s32[]{:S(2)}) async-start(), calls=%async_computation.8 | async-start | bytes 2621440 | tf_op jit(solution)/shard_map/all_gather | solution.py:61
  7.3 156.1 %reduce-scatter.5.cloned.1.call-start = ((), (), s32[]{:S(2)}) async-start(), calls=%async_computation.4 | async-start | bytes 655360 | tf_op jit(solution)/shard_map/reduce_scatter | solution.py:70
  57.3 11.4 %copy-start.3 = (s32[12]{0:T(128)S(1)}, s32[12]{0:T(128)}, u32[]{:S(2)}) copy-start(s32[12]{0:T(128)} %param.12) | copy-start | bytes 148
  57.3 11.5 %copy-start.7 = (s32[12]{0:T(128)S(1)}, s32[12]{0:T(128)}, u32[]{:S(2)}) copy-start(s32[12]{0:T(128)} %param.13) | copy-start | bytes 148
  57.3 47.2 %collective-permute-start.1 = (bf16[8,1,4,256,128]{4,3,2,1,0:T(8,128)(2,1)}, bf16[8,1,4,256,128]{4,3,2,1,0:T(8,128)(2,1)}, u32[]{:S(2)}, u32[]{:S(2)}) collective-permute-start(bf16[8,1,4,256,128]{4,3,2,1,0:T(8,128)(2,1)} %bitcast.126), channel_id=1, source_target_pairs={{4,0},{8,4},{12,8},{16,12},{20,16},{24,20},{28,24},{0,28},{5,1},{9... | collective-permute-start | bytes 6291464 | tf_op jit(solution)/shard_map/ppermute | solution.py:16
  59.0 47.5 %collective-permute-start = (bf16[8,1,4,256,128]{4,3,2,1,0:T(8,128)(2,1)}, bf16[8,1,4,256,128]{4,3,2,1,0:T(8,128)(2,1)}, u32[]{:S(2)}, u32[]{:S(2)}) collective-permute-start(bf16[8,1,4,256,128]{4,3,2,1,0:T(8,128)(2,1)} %bitcast.127), channel_id=1, source_target_pairs={{0,4},{4,8},{8,12},{12,16},{16,20},{20,24},{24,28},{28,0},{1,5},{5... | collective-permute-start | bytes 6291464 | tf_op jit(solution)/shard_map/ppermute | solution.py:13
  68.8 51.1 %copy-start.8 = (pred[12]{0:T(512)(128)(4,1)}, pred[12]{0:T(512)(128)(4,1)S(1)}, u32[]{:S(2)}) copy-start(pred[12]{0:T(512)(128)(4,1)S(1)} %compare_and_fusion) | copy-start | bytes 40
  68.9 51.0 %copy-start.4 = (bf16[8,12]{0,1:T(8,128)(2,1)}, bf16[8,12]{0,1:T(8,128)(2,1)S(1)}, u32[]{:S(2)}) copy-start(bf16[8,12]{0,1:T(8,128)(2,1)S(1)} %compare_convert_fusion) | copy-start | bytes 580
  132.0 11.6 %copy-start.1 = (bf16[8,256,128]{2,1,0:T(8,128)(2,1)S(1)}, bf16[8,256,128]{2,1,0:T(8,128)(2,1)}, u32[]{:S(2)}) copy-start(bf16[8,256,128]{2,1,0:T(8,128)(2,1)} %param.8) | copy-start | bytes 1572868
  132.0 31.4 %copy-start.2 = (bf16[4,256,128]{2,1,0:T(8,128)(2,1)S(1)}, bf16[4,256,128]{2,1,0:T(8,128)(2,1)}, u32[]{:S(2)}) copy-start(bf16[4,256,128]{2,1,0:T(8,128)(2,1)} %param.9) | copy-start | bytes 786436
  133.6 8.8 %collective-permute-start.3 = (bf16[4,256,128]{2,0,1:T(4,128)(2,1)S(1)}, bf16[4,256,128]{2,0,1:T(4,128)(2,1)S(1)}, u32[]{:S(2)}, u32[]{:S(2)}) collective-permute-start(bf16[4,256,128]{2,0,1:T(4,128)(2,1)S(1)} %get-tuple-element.13), channel_id=1, source_target_pairs={{28,0},{0,4},{4,8},{8,12},{12,16},{16,20},{20,24},{24,28},{29,1},{... | collective-permute-start | bytes 786440 | tf_op jit(solution)/shard_map/ppermute | solution.py:24
  133.7 8.8 %collective-permute-start.2 = (bf16[4,256,128]{2,0,1:T(4,128)(2,1)S(1)}, bf16[4,256,128]{2,0,1:T(4,128)(2,1)S(1)}, u32[]{:S(2)}, u32[]{:S(2)}) collective-permute-start(bf16[4,256,128]{2,0,1:T(4,128)(2,1)S(1)} %get-tuple-element.12), channel_id=1, source_target_pairs={{4,0},{8,4},{12,8},{16,12},{20,16},{24,20},{28,24},{0,28},{5,1},{9... | collective-permute-start | bytes 786440 | tf_op jit(solution)/shard_map/ppermute | solution.py:24
  143.5 66.0 %all-gather.11.cloned.1.call-start = ((), (), s32[]{:S(2)}) async-start(), calls=%async_computation.9 | async-start | bytes 2621440 | tf_op jit(solution)/shard_map/all_gather | solution.py:61
  165.5 150.0 %reduce-scatter.7.cloned.1.call-start = ((), (), s32[]{:S(2)}) async-start(), calls=%async_computation.5 | async-start | bytes 655360 | tf_op jit(solution)/shard_map/reduce_scatter | solution.py:70
  209.5 47.7 %collective-permute-start.5 = (bf16[8,1,4,256,128]{4,3,2,1,0:T(8,128)(2,1)}, bf16[8,1,4,256,128]{4,3,2,1,0:T(8,128)(2,1)}, u32[]{:S(2)}, u32[]{:S(2)}) collective-permute-start(bf16[8,1,4,256,128]{4,3,2,1,0:T(8,128)(2,1)} %bitcast.132), channel_id=1, source_target_pairs={{4,0},{8,4},{12,8},{16,12},{20,16},{24,20},{28,24},{0,28},{5,1},{9... | collective-permute-start | bytes 6291464 | tf_op jit(solution)/shard_map/ppermute | solution.py:16
  211.2 47.5 %collective-permute-start.4 = (bf16[8,1,4,256,128]{4,3,2,1,0:T(8,128)(2,1)}, bf16[8,1,4,256,128]{4,3,2,1,0:T(8,128)(2,1)}, u32[]{:S(2)}, u32[]{:S(2)}) collective-permute-start(bf16[8,1,4,256,128]{4,3,2,1,0:T(8,128)(2,1)} %bitcast.133), channel_id=1, source_target_pairs={{0,4},{4,8},{8,12},{12,16},{16,20},{20,24},{24,28},{28,0},{1,5},{5... | collective-permute-start | bytes 6291464 | tf_op jit(solution)/shard_map/ppermute | solution.py:13
  265.1 6.9 %copy-start.5 = (bf16[8,12]{0,1:T(8,128)(2,1)S(1)}, bf16[8,12]{0,1:T(8,128)(2,1)}, u32[]{:S(2)}) copy-start(bf16[8,12]{0,1:T(8,128)(2,1)} %copy-done.4) | copy-start | bytes 580
  265.1 6.9 %copy-start.9 = (pred[12]{0:T(512)(128)(4,1)S(1)}, pred[12]{0:T(512)(128)(4,1)}, u32[]{:S(2)}) copy-start(pred[12]{0:T(512)(128)(4,1)} %copy-done.8) | copy-start | bytes 40
  285.8 8.8 %collective-permute-start.7 = (bf16[4,256,128]{2,0,1:T(4,128)(2,1)S(1)}, bf16[4,256,128]{2,0,1:T(4,128)(2,1)S(1)}, u32[]{:S(2)}, u32[]{:S(2)}) collective-permute-start(bf16[4,256,128]{2,0,1:T(4,128)(2,1)S(1)} %get-tuple-element.11), channel_id=1, source_target_pairs={{28,0},{0,4},{4,8},{8,12},{12,16},{16,20},{20,24},{24,28},{29,1},{... | collective-permute-start | bytes 786440 | tf_op jit(solution)/shard_map/ppermute | solution.py:24
  285.8 8.8 %collective-permute-start.6 = (bf16[4,256,128]{2,0,1:T(4,128)(2,1)S(1)}, bf16[4,256,128]{2,0,1:T(4,128)(2,1)S(1)}, u32[]{:S(2)}, u32[]{:S(2)}) collective-permute-start(bf16[4,256,128]{2,0,1:T(4,128)(2,1)S(1)} %get-tuple-element.10), channel_id=1, source_target_pairs={{4,0},{8,4},{12,8},{16,12},{20,16},{24,20},{28,24},{0,28},{5,1},{9... | collective-permute-start | bytes 786440 | tf_op jit(solution)/shard_map/ppermute | solution.py:24
  295.7 65.9 %all-gather.13.cloned.1.call-start = ((), (), s32[]{:S(2)}) async-start(), calls=%async_computation.10 | async-start | bytes 2621440 | tf_op jit(solution)/shard_map/all_gather | solution.py:61
  317.6 149.9 %reduce-scatter.9.cloned.1.call-start = ((), (), s32[]{:S(2)}) async-start(), calls=%async_computation.6 | async-start | bytes 655360 | tf_op jit(solution)/shard_map/reduce_scatter | solution.py:70
  361.6 47.4 %collective-permute-start.9 = (bf16[8,1,4,256,128]{4,3,2,1,0:T(8,128)(2,1)}, bf16[8,1,4,256,128]{4,3,2,1,0:T(8,128)(2,1)}, u32[]{:S(2)}, u32[]{:S(2)}) collective-permute-start(bf16[8,1,4,256,128]{4,3,2,1,0:T(8,128)(2,1)} %bitcast.135), channel_id=1, source_target_pairs={{4,0},{8,4},{12,8},{16,12},{20,16},{24,20},{28,24},{0,28},{5,1},{9... | collective-permute-start | bytes 6291464 | tf_op jit(solution)/shard_map/ppermute | solution.py:16
  363.3 47.5 %collective-permute-start.8 = (bf16[8,1,4,256,128]{4,3,2,1,0:T(8,128)(2,1)}, bf16[8,1,4,256,128]{4,3,2,1,0:T(8,128)(2,1)}, u32[]{:S(2)}, u32[]{:S(2)}) collective-permute-start(bf16[8,1,4,256,128]{4,3,2,1,0:T(8,128)(2,1)} %bitcast.136), channel_id=1, source_target_pairs={{0,4},{4,8},{8,12},{12,16},{16,20},{20,24},{24,28},{28,0},{1,5},{5... | collective-permute-start | bytes 6291464 | tf_op jit(solution)/shard_map/ppermute | solution.py:13
  417.3 6.9 %copy-start.6 = (bf16[8,12]{0,1:T(8,128)(2,1)S(1)}, bf16[8,12]{0,1:T(8,128)(2,1)}, u32[]{:S(2)}) copy-start(bf16[8,12]{0,1:T(8,128)(2,1)} %copy-done.4) | copy-start | bytes 580
  417.3 6.9 %copy-start.10 = (pred[12]{0:T(512)(128)(4,1)S(1)}, pred[12]{0:T(512)(128)(4,1)}, u32[]{:S(2)}) copy-start(pred[12]{0:T(512)(128)(4,1)} %copy-done.8) | copy-start | bytes 40
  437.9 8.8 %collective-permute-start.11 = (bf16[4,256,128]{2,0,1:T(4,128)(2,1)S(1)}, bf16[4,256,128]{2,0,1:T(4,128)(2,1)S(1)}, u32[]{:S(2)}, u32[]{:S(2)}) collective-permute-start(bf16[4,256,128]{2,0,1:T(4,128)(2,1)S(1)} %get-tuple-element.9), channel_id=1, source_target_pairs={{28,0},{0,4},{4,8},{8,12},{12,16},{16,20},{20,24},{24,28},{29,1},{... | collective-permute-start | bytes 786440 | tf_op jit(solution)/shard_map/ppermute | solution.py:24
  438.0 8.8 %collective-permute-start.10 = (bf16[4,256,128]{2,0,1:T(4,128)(2,1)S(1)}, bf16[4,256,128]{2,0,1:T(4,128)(2,1)S(1)}, u32[]{:S(2)}, u32[]{:S(2)}) collective-permute-start(bf16[4,256,128]{2,0,1:T(4,128)(2,1)S(1)} %get-tuple-element.8), channel_id=1, source_target_pairs={{4,0},{8,4},{12,8},{16,12},{20,16},{24,20},{28,24},{0,28},{5,1},{9... | collective-permute-start | bytes 786440 | tf_op jit(solution)/shard_map/ppermute | solution.py:24
  447.8 65.7 %all-gather.15.cloned.1.call-start = ((), (), s32[]{:S(2)}) async-start(), calls=%async_computation.11 | async-start | bytes 2621440 | tf_op jit(solution)/shard_map/all_gather | solution.py:61
  469.5 149.7 %reduce-scatter.11.cloned.1.call-start = ((), (), s32[]{:S(2)}) async-start(), calls=%async_computation.7 | async-start | bytes 655360 | tf_op jit(solution)/shard_map/reduce_scatter | solution.py:70
  513.6 47.4 %collective-permute-start.13 = (bf16[8,1,4,256,128]{4,3,2,1,0:T(8,128)(2,1)}, bf16[8,1,4,256,128]{4,3,2,1,0:T(8,128)(2,1)}, u32[]{:S(2)}, u32[]{:S(2)}) collective-permute-start(bf16[8,1,4,256,128]{4,3,2,1,0:T(8,128)(2,1)} %bitcast.129), channel_id=1, source_target_pairs={{4,0},{8,4},{12,8},{16,12},{20,16},{24,20},{28,24},{0,28},{5,1},{9... | collective-permute-start | bytes 6291464 | tf_op jit(solution)/shard_map/ppermute | solution.py:16
  515.2 47.5 %collective-permute-start.12 = (bf16[8,1,4,256,128]{4,3,2,1,0:T(8,128)(2,1)}, bf16[8,1,4,256,128]{4,3,2,1,0:T(8,128)(2,1)}, u32[]{:S(2)}, u32[]{:S(2)}) collective-permute-start(bf16[8,1,4,256,128]{4,3,2,1,0:T(8,128)(2,1)} %bitcast.130), channel_id=1, source_target_pairs={{0,4},{4,8},{8,12},{12,16},{16,20},{20,24},{24,28},{28,0},{1,5},{5... | collective-permute-start | bytes 6291464 | tf_op jit(solution)/shard_map/ppermute | solution.py:13
  589.8 8.8 %collective-permute-start.15 = (bf16[4,256,128]{2,0,1:T(4,128)(2,1)S(1)}, bf16[4,256,128]{2,0,1:T(4,128)(2,1)S(1)}, u32[]{:S(2)}, u32[]{:S(2)}) collective-permute-start(bf16[4,256,128]{2,0,1:T(4,128)(2,1)S(1)} %get-tuple-element.7), channel_id=1, source_target_pairs={{28,0},{0,4},{4,8},{8,12},{12,16},{16,20},{20,24},{24,28},{29,1},{... | collective-permute-start | bytes 786440 | tf_op jit(solution)/shard_map/ppermute | solution.py:24
  589.9 8.8 %collective-permute-start.14 = (bf16[4,256,128]{2,0,1:T(4,128)(2,1)S(1)}, bf16[4,256,128]{2,0,1:T(4,128)(2,1)S(1)}, u32[]{:S(2)}, u32[]{:S(2)}) collective-permute-start(bf16[4,256,128]{2,0,1:T(4,128)(2,1)S(1)} %get-tuple-element.6), channel_id=1, source_target_pairs={{4,0},{8,4},{12,8},{16,12},{20,16},{24,20},{28,24},{0,28},{5,1},{9... | collective-permute-start | bytes 786440 | tf_op jit(solution)/shard_map/ppermute | solution.py:24
Sparse Core Ops, SparseCore 0:
  8.9 48.3 all-gather.8
  143.6 19.6 reduce-scatter.4
  165.6 43.8 all-gather.10
  295.8 19.5 reduce-scatter.6
  317.7 43.9 all-gather.12
  448.0 19.4 reduce-scatter.8
  469.7 43.8 all-gather.14
  599.9 19.3 reduce-scatter.10
where the time goes:
time: 636 us; the launch traced here: 628 us
  waiting for transfers between devices  430 us (68%)
  matrix products  88.6 us (14%)
  local copies, waits for them, and re-layouts  46.8 us (7%)
  other arithmetic  30.2 us (5%)
  starting transfers between devices  18.5 us (3%)
  between operations  14.2 us (2%)
    all_gather x4, waiting for transfers between devices, on_device(): stacked = lax.all_gather(recent[:, None, None], 'cuts', axis=2, tiled=True)  180 us
    ppermute x4, waiting for transfers between devices, padded(): lax.ppermute(lax.slice_in_dim(block, 0, width, axis=dim), axis, backward)  139 us
    reduce_scatter x4, waiting for transfers between devices, on_device(): lax.psum_scatter(grouped[1] + from_above + from_below, 'cuts', scatter_di...  78.4 us
    dot_general x4, matrix products, near_field(): jnp.einsum('plij,lpjr->ir', lag_kernels, partner_hist, preferred_element_...  48.4 us
    dot_general x4, matrix products, near_field(): jnp.einsum('plij,plir->pjr', lag_kernels, own_hist, preferred_element_typ...  30.4 us
    gather x4, local copies, waits for them, and re-layouts, near_field(): partner_hist = jnp.take(window, pair_partner, axis=1)  27.7 us
    concatenate x4, other arithmetic, padded(): block = jnp.concatenate([low, block, high], axis=dim)  25.8 us
    ppermute x8, waiting for transfers between devices, shifted(): return lax.ppermute(block, axis, route)  24.6 us
  transfers between devices with their start and end apart: 24, of which 20 were waited for; matrix products, arithmetic and copies ran while one was open for 7% of the time, Pallas kernels for 0%

commit v1 on v0

--- a/solution.py
+++ b/solution.py
@@ -58,7 +58,9 @@
     window = history
     outputs = []
     for step_now in range(step_total):
-        stacked = lax.all_gather(recent[:, None, None], "cuts", axis=2, tiled=True)
+        block_2 = recent[:, None, None]
+        sent = jnp.stack([block_2] * lax.axis_size("cuts"))
+        stacked = jnp.concatenate(lax.all_to_all(sent, "cuts", 0, 0), axis=2)
         bordered = padded(stacked, (("region", 1),), 1)
         window = bordered.reshape(lag_total, 3 * cut_count, panel_count, column_count)
         partial_field = near_field(

time: 636 us -> 663 us (1.042)
  blocking collectives: 0 us -> 150 us
  waiting for transfers between devices: 430 us -> 305 us
  other arithmetic: 30.2 us -> 16.7 us
  local copies, waits for them, and re-layouts: 46.8 us -> 59 us
    all_gather x4 -> x0, waiting for transfers between devices: 180 us -> none  [on_device(): stacked = lax.all_gather(recent[:, None, None], 'cuts', axis=2, tiled=True)]
    all_to_all x0 -> x3, blocking collectives: none -> 150 us  [on_device(): stacked = jnp.concatenate(lax.all_to_all(sent, 'cuts', 0, 0), axis=2)]
    all_to_all x0 -> x1, waiting for transfers between devices: none -> 48 us  [on_device(): stacked = jnp.concatenate(lax.all_to_all(sent, 'cuts', 0, 0), axis=2)]
    concatenate x0 -> x4, local copies, waits for them, and re-layouts: none -> 12.2 us  [padded(): block = jnp.concatenate([low, block, high], axis=dim)]
    concatenate x4, other arithmetic: 25.8 us -> 15.3 us  [padded(): block = jnp.concatenate([low, block, high], axis=dim)]
  transfers between devices with their start and end apart: 24 -> 21, of which waited for: 20 -> 17; matrix products, arithmetic and copies ran while one was open for 7% -> 6% of each run, Pallas kernels for 0% -> 0%
where the time goes in v1:
time: 663 us; the launch traced here: 654 us
  waiting for transfers between devices  305 us (46%)
  blocking collectives  150 us (23%)
  matrix products  88.5 us (13%)
  local copies, waits for them, and re-layouts  59 us (9%)
  starting transfers between devices  20.7 us (3%)
  other arithmetic  16.7 us (3%)
  between operations  13.8 us (2%)
    all_to_all x3, blocking collectives, on_device(): stacked = jnp.concatenate(lax.all_to_all(sent, 'cuts', 0, 0), axis=2)  150 us
    ppermute x4, waiting for transfers between devices, padded(): lax.ppermute(lax.slice_in_dim(block, 0, width, axis=dim), axis, backward)  142 us
    reduce_scatter x4, waiting for transfers between devices, on_device(): lax.psum_scatter(grouped[1] + from_above + from_below, 'cuts', scatter_di...  76.7 us
    dot_general x4, matrix products, near_field(): jnp.einsum('plij,lpjr->ir', lag_kernels, partner_hist, preferred_element_...  48.3 us
    all_to_all x1, waiting for transfers between devices, on_device(): stacked = jnp.concatenate(lax.all_to_all(sent, 'cuts', 0, 0), axis=2)  48 us
    dot_general x4, matrix products, near_field(): jnp.einsum('plij,plir->pjr', lag_kernels, own_hist, preferred_element_typ...  30.4 us
    gather x4, local copies, waits for them, and re-layouts, near_field(): partner_hist = jnp.take(window, pair_partner, axis=1)  27.5 us
    ppermute x8, waiting for transfers between devices, shifted(): return lax.ppermute(block, axis, route)  27.2 us
  transfers between devices with their start and end apart: 21, of which 17 were waited for; matrix products, arithmetic and copies ran while one was open for 6% of the time, Pallas kernels for 0%

profile of v1, /device:TPU:0, one launch (start us, length us, event | category | flops | bytes accessed | tf_op | source)
XLA Modules:
  0.0 654.5 jit_solution(7967869070600802200)
XLA Ops:
  6.5 2.9 stack.27
  9.5 6.3 all-to-all-start
  16.1 48.0 %all-to-all-done = bf16[4,8,1,1,256,128]{5,4,1,3,2,0:T(8,128)(2,1)} async-done(((bf16[4,8,1,1,256,128]{5,4,1,3,2,0:T(8,128)(2,1)}), bf16[4,8,1,1,256,128]{5,4,1,3,2,0:T(8,128)(2,1)}, u32[]{:S(2)}, u32[]{:S(2)}) %all-to-all-start) | async-done | bytes 2097184 | tf_op jit(solution)/shard_map/all_to_all | solution.py:63
  64.1 1.2 collective-permute-start.1
  65.3 7.6 %fusion.28 = f32[12,256,128]{1,2,0:T(8,128)} fusion(bf16[12,8,256,256]{3,2,1,0:T(8,128)(2,1)} %param.11, bf16[8,256,128]{1,2,0:T(8,128)(2,1)S(1)} %copy.43, bf16[12,8]{1,0:T(8,128)(2,1)S(1)} %compare_convert_fusion.1), kind=kOutput, calls=%fused_computation.44 | convolution fusion | flops 1613758464 | bytes 14680256 | tf_op jit(solution)/shard_map/plij,plir->pjr/dot_general | solution.py:39
  72.9 2.1 copy.44
  75.2 36.2 %collective-permute-done.1 = bf16[8,1,4,256,128]{4,3,0,2,1:T(8,128)(2,1)} collective-permute-done((bf16[8,1,4,256,128]{4,3,0,2,1:T(8,128)(2,1)}, bf16[8,1,4,256,128]{4,3,0,2,1:T(8,128)(2,1)}, u32[]{:S(2)}, u32[]{:S(2)}) %collective-permute-start.1) | collective-permute-done | bytes 2097184 | tf_op jit(solution)/shard_map/ppermute | solution.py:16
  111.4 2.0 collective-permute-done
  113.4 3.8 pad_maximum_fusion
  117.2 3.1 copy.45
  120.3 6.9 %gather_fusion = bf16[12,8,256,128]{3,2,1,0:T(8,128)(2,1)} fusion(bf16[8,12,256,128]{3,2,1,0:T(8,128)(2,1)} %bitcast.131, s32[1024]{0:T(1024)S(1)} %pad_clamp_fusion), kind=kCustom, calls=%fused_computation.clone | custom fusion | bytes 12582960 | tf_op jit(solution)/shard_map/jit(_take)/gather | solution.py:33
  127.1 12.1 %fusion.40 = f32[256,128]{0,1:T(8,128)S(1)} fusion(bf16[12,8,256,256]{3,2,1,0:T(8,128)(2,1)} %param.11, bf16[12,8,256,128]{3,2,1,0:T(8,128)(2,1)} %gather_fusion, pred[12]{0:T(512)(128)(4,1)S(1)} %compare_and_fusion, bf16[8,12]{0,1:T(8,128)(2,1)S(1)} %compare_convert_fusion), kind=kOutput, calls=%fused_computation.48 | convolution fusion | flops 1616904192 | bytes 19005644 | tf_op jit(solution)/shard_map/plij,lpjr->ir/dot_general | solution.py:35
  139.3 1.3 fusion.95
  140.9 2.6 collective-permute-start.2
  143.6 6.7 %collective-permute-done.3 = bf16[4,256,128]{2,0,1:T(4,128)(2,1)S(1)} collective-permute-done((bf16[4,256,128]{2,0,1:T(4,128)(2,1)S(1)}, bf16[4,256,128]{2,0,1:T(4,128)(2,1)S(1)}, u32[]{:S(2)}, u32[]{:S(2)}) %collective-permute-start.3) | collective-permute-done | bytes 262176 | tf_op jit(solution)/shard_map/ppermute | solution.py:24
  150.5 0.8 copy.49
  151.5 19.2 %reduce-scatter.5.cloned.1.call-done = f32[1,256,128]{2,1,0:T(8,128)} async-done(((f32[4,256,128]{2,1,0:T(8,128)}), f32[1,256,128]{2,1,0:T(8,128)}) %reduce-scatter.5.cloned.1.call-update) | async-done | bytes 131088 | tf_op jit(solution)/shard_map/reduce_scatter | solution.py:72
  170.7 1.1 fusion.60
  172.5 50.1 %all_to_all.20 = bf16[4,8,1,1,256,128]{5,4,1,3,2,0:T(8,128)(2,1)} all-to-all(bf16[4,8,1,1,256,128]{5,4,1,3,2,0:T(8,128)(2,1)S(1)} %stack.29), channel_id=1, replica_groups=mesh['region'=8,'cuts'=4] {'cuts'}, dimensions={0} | all-to-all | bytes 4194304 | tf_op jit(solution)/shard_map/all_to_all | solution.py:63
  223.7 7.6 %fusion.31 = f32[12,256,128]{1,2,0:T(8,128)} fusion(bf16[12,8,256,256]{3,2,1,0:T(8,128)(2,1)} %param.11, bf16[8,256,128]{1,2,0:T(8,128)(2,1)S(1)} %copy.51, bf16[12,8]{1,0:T(8,128)(2,1)S(1)} %compare_convert_fusion.1), kind=kOutput, calls=%fused_computation.45 | convolution fusion | flops 1613758464 | bytes 14680256 | tf_op jit(solution)/shard_map/plij,plir->pjr/dot_general | solution.py:39
  231.3 2.1 copy.52
  233.5 35.0 %collective-permute-done.5 = bf16[8,1,4,256,128]{4,3,0,2,1:T(8,128)(2,1)} collective-permute-done((bf16[8,1,4,256,128]{4,3,0,2,1:T(8,128)(2,1)}, bf16[8,1,4,256,128]{4,3,0,2,1:T(8,128)(2,1)}, u32[]{:S(2)}, u32[]{:S(2)}) %collective-permute-start.5) | collective-permute-done | bytes 2097184 | tf_op jit(solution)/shard_map/ppermute | solution.py:16
  268.5 3.2 collective-permute-done.4
  271.7 3.8 pad_maximum_fusion.1
  275.5 3.1 copy.53
  278.6 6.9 %gather_fusion.1 = bf16[12,8,256,128]{3,2,1,0:T(8,128)(2,1)} fusion(bf16[8,12,256,128]{3,2,1,0:T(8,128)(2,1)} %bitcast.132, s32[1024]{0:T(1024)S(1)} %pad_clamp_fusion), kind=kCustom, calls=%fused_computation.1.clone | custom fusion | bytes 12582960 | tf_op jit(solution)/shard_map/jit(_take)/gather | solution.py:33
  285.5 12.1 %fusion.45 = f32[256,128]{0,1:T(8,128)S(1)} fusion(bf16[12,8,256,256]{3,2,1,0:T(8,128)(2,1)} %param.11, bf16[12,8,256,128]{3,2,1,0:T(8,128)(2,1)} %gather_fusion.1, pred[12]{0:T(512)(128)(4,1)S(1)} %copy-done.9, bf16[8,12]{0,1:T(8,128)(2,1)S(1)} %copy-done.5), kind=kOutput, calls=%fused_computation.49 | convolution fusion | flops 1616904192 | bytes 19005644 | tf_op jit(solution)/shard_map/plij,lpjr->ir/dot_general | solution.py:35
  297.7 1.4 fusion.96
  299.3 2.6 collective-permute-start.6
  301.9 6.8 %collective-permute-done.7 = bf16[4,256,128]{2,0,1:T(4,128)(2,1)S(1)} collective-permute-done((bf16[4,256,128]{2,0,1:T(4,128)(2,1)S(1)}, bf16[4,256,128]{2,0,1:T(4,128)(2,1)S(1)}, u32[]{:S(2)}, u32[]{:S(2)}) %collective-permute-start.7) | collective-permute-done | bytes 262176 | tf_op jit(solution)/shard_map/ppermute | solution.py:24
  309.0 0.8 copy.57
  309.9 19.1 %reduce-scatter.7.cloned.1.call-done = f32[1,256,128]{2,1,0:T(8,128)} async-done(((f32[4,256,128]{2,1,0:T(8,128)}), f32[1,256,128]{2,1,0:T(8,128)}) %reduce-scatter.7.cloned.1.call-update) | async-done | bytes 131088 | tf_op jit(solution)/shard_map/reduce_scatter | solution.py:72
  329.1 1.1 fusion.61
  330.8 50.1 %all_to_all.21 = bf16[4,8,1,1,256,128]{5,4,1,3,2,0:T(8,128)(2,1)} all-to-all(bf16[4,8,1,1,256,128]{5,4,1,3,2,0:T(8,128)(2,1)S(1)} %stack.31), channel_id=1, replica_groups=mesh['region'=8,'cuts'=4] {'cuts'}, dimensions={0} | all-to-all | bytes 4194304 | tf_op jit(solution)/shard_map/all_to_all | solution.py:63
  381.8 7.6 %fusion.34 = f32[12,256,128]{1,2,0:T(8,128)} fusion(bf16[12,8,256,256]{3,2,1,0:T(8,128)(2,1)} %param.11, bf16[8,256,128]{1,2,0:T(8,128)(2,1)S(1)} %copy.59, bf16[12,8]{1,0:T(8,128)(2,1)S(1)} %compare_convert_fusion.1), kind=kOutput, calls=%fused_computation.46 | convolution fusion | flops 1613758464 | bytes 14680256 | tf_op jit(solution)/shard_map/plij,plir->pjr/dot_general | solution.py:39
  389.4 2.1 copy.60
  391.5 35.7 %collective-permute-done.9 = bf16[8,1,4,256,128]{4,3,0,2,1:T(8,128)(2,1)} collective-permute-done((bf16[8,1,4,256,128]{4,3,0,2,1:T(8,128)(2,1)}, bf16[8,1,4,256,128]{4,3,0,2,1:T(8,128)(2,1)}, u32[]{:S(2)}, u32[]{:S(2)}) %collective-permute-start.9) | collective-permute-done | bytes 2097184 | tf_op jit(solution)/shard_map/ppermute | solution.py:16
  427.2 2.9 collective-permute-done.8
  430.1 3.8 pad_maximum_fusion.2
  433.9 3.0 copy.61
  437.0 6.9 %gather_fusion.2 = bf16[12,8,256,128]{3,2,1,0:T(8,128)(2,1)} fusion(bf16[8,12,256,128]{3,2,1,0:T(8,128)(2,1)} %bitcast.133, s32[1024]{0:T(1024)S(1)} %pad_clamp_fusion), kind=kCustom, calls=%fused_computation.2.clone | custom fusion | bytes 12582960 | tf_op jit(solution)/shard_map/jit(_take)/gather | solution.py:33
  443.9 12.1 %fusion.50 = f32[256,128]{0,1:T(8,128)S(1)} fusion(bf16[12,8,256,256]{3,2,1,0:T(8,128)(2,1)} %param.11, bf16[12,8,256,128]{3,2,1,0:T(8,128)(2,1)} %gather_fusion.2, pred[12]{0:T(512)(128)(4,1)S(1)} %copy-done.10, bf16[8,12]{0,1:T(8,128)(2,1)S(1)} %copy-done.6), kind=kOutput, calls=%fused_computation.50 | convolution fusion | flops 1616904192 | bytes 19005644 | tf_op jit(solution)/shard_map/plij,lpjr->ir/dot_general | solution.py:35
  456.1 1.4 fusion.97
  457.6 2.6 collective-permute-start.10
  460.3 6.8 %collective-permute-done.11 = bf16[4,256,128]{2,0,1:T(4,128)(2,1)S(1)} collective-permute-done((bf16[4,256,128]{2,0,1:T(4,128)(2,1)S(1)}, bf16[4,256,128]{2,0,1:T(4,128)(2,1)S(1)}, u32[]{:S(2)}, u32[]{:S(2)}) %collective-permute-start.11) | collective-permute-done | bytes 262176 | tf_op jit(solution)/shard_map/ppermute | solution.py:24
  467.3 0.8 copy.65
  468.3 19.1 %reduce-scatter.9.cloned.1.call-done = f32[1,256,128]{2,1,0:T(8,128)} async-done(((f32[4,256,128]{2,1,0:T(8,128)}), f32[1,256,128]{2,1,0:T(8,128)}) %reduce-scatter.9.cloned.1.call-update) | async-done | bytes 131088 | tf_op jit(solution)/shard_map/reduce_scatter | solution.py:72
  487.4 1.1 fusion.62
  489.2 50.1 %all_to_all.22 = bf16[4,8,1,1,256,128]{5,4,1,3,2,0:T(8,128)(2,1)} all-to-all(bf16[4,8,1,1,256,128]{5,4,1,3,2,0:T(8,128)(2,1)S(1)} %stack.33), channel_id=1, replica_groups=mesh['region'=8,'cuts'=4] {'cuts'}, dimensions={0} | all-to-all | bytes 4194304 | tf_op jit(solution)/shard_map/all_to_all | solution.py:63
  540.2 7.6 %fusion.37 = f32[12,256,128]{1,2,0:T(8,128)} fusion(bf16[12,8,256,256]{3,2,1,0:T(8,128)(2,1)} %param.11, bf16[8,256,128]{1,2,0:T(8,128)(2,1)S(1)} %copy.67, bf16[12,8]{1,0:T(8,128)(2,1)S(1)} %compare_convert_fusion.1), kind=kOutput, calls=%fused_computation.47 | convolution fusion | flops 1613758464 | bytes 14680256 | tf_op jit(solution)/shard_map/plij,plir->pjr/dot_general | solution.py:39
  547.8 2.1 copy.68
  549.9 35.5 %collective-permute-done.13 = bf16[8,1,4,256,128]{4,3,0,2,1:T(8,128)(2,1)} collective-permute-done((bf16[8,1,4,256,128]{4,3,0,2,1:T(8,128)(2,1)}, bf16[8,1,4,256,128]{4,3,0,2,1:T(8,128)(2,1)}, u32[]{:S(2)}, u32[]{:S(2)}) %collective-permute-start.13) | collective-permute-done | bytes 2097184 | tf_op jit(solution)/shard_map/ppermute | solution.py:16
  585.5 3.0 collective-permute-done.12
  588.4 3.8 pad_maximum_fusion.3
  592.3 3.1 copy.69
  595.3 6.9 %gather_fusion.3 = bf16[12,8,256,128]{3,2,1,0:T(8,128)(2,1)} fusion(bf16[8,12,256,128]{3,2,1,0:T(8,128)(2,1)} %bitcast.130, s32[1024]{0:T(1024)S(1)} %pad_clamp_fusion), kind=kCustom, calls=%fused_computation.3.clone | custom fusion | bytes 12582960 | tf_op jit(solution)/shard_map/jit(_take)/gather | solution.py:33
  602.2 12.1 %fusion.55 = f32[256,128]{0,1:T(8,128)S(1)} fusion(bf16[12,8,256,256]{3,2,1,0:T(8,128)(2,1)} %param.11, bf16[12,8,256,128]{3,2,1,0:T(8,128)(2,1)} %gather_fusion.3, pred[12]{0:T(512)(128)(4,1)S(1)} %copy-done.10, bf16[8,12]{0,1:T(8,128)(2,1)S(1)} %copy-done.6), kind=kOutput, calls=%fused_computation.51 | convolution fusion | flops 1616904192 | bytes 19005644 | tf_op jit(solution)/shard_map/plij,lpjr->ir/dot_general | solution.py:35
  614.4 1.4 fusion.98
  616.0 2.6 collective-permute-start.14
  618.6 6.8 %collective-permute-done.15 = bf16[4,256,128]{2,0,1:T(4,128)(2,1)S(1)} collective-permute-done((bf16[4,256,128]{2,0,1:T(4,128)(2,1)S(1)}, bf16[4,256,128]{2,0,1:T(4,128)(2,1)S(1)}, u32[]{:S(2)}, u32[]{:S(2)}) %collective-permute-start.15) | collective-permute-done | bytes 262176 | tf_op jit(solution)/shard_map/ppermute | solution.py:24
  625.7 0.8 copy.73
  626.5 19.2 %reduce-scatter.11.cloned.1.call-done = f32[1,256,128]{2,1,0:T(8,128)} async-done(((f32[4,256,128]{2,1,0:T(8,128)}), f32[1,256,128]{2,1,0:T(8,128)}) %reduce-scatter.11.cloned.1.call-update) | async-done | bytes 131088 | tf_op jit(solution)/shard_map/reduce_scatter | solution.py:72
  645.7 1.1 fusion.63
  646.9 0.8 copy.74
  (81 shorter events, 7.7 us)
Async XLA Ops:
  6.5 164.2 %copy-start = (bf16[256,256]{1,0:T(8,128)(2,1)S(1)}, bf16[256,256]{1,0:T(8,128)(2,1)}, u32[]{:S(2)}) copy-start(bf16[256,256]{1,0:T(8,128)(2,1)} %param.10) | copy-start | bytes 393220
  6.5 9.3 %copy-start.1 = (bf16[8,256,128]{2,1,0:T(8,128)(2,1)S(1)}, bf16[8,256,128]{2,1,0:T(8,128)(2,1)}, u32[]{:S(2)}) copy-start(bf16[8,256,128]{2,1,0:T(8,128)(2,1)} %param.8) | copy-start | bytes 1572868
  6.5 9.5 %copy-start.7 = (s32[12]{0:T(128)S(1)}, s32[12]{0:T(128)}, u32[]{:S(2)}) copy-start(s32[12]{0:T(128)} %param.13) | copy-start | bytes 148
  9.5 54.6 %all-to-all-start = ((bf16[4,8,1,1,256,128]{5,4,1,3,2,0:T(8,128)(2,1)}), bf16[4,8,1,1,256,128]{5,4,1,3,2,0:T(8,128)(2,1)}, u32[]{:S(2)}, u32[]{:S(2)}) async-start(bf16[4,8,1,1,256,128]{5,4,1,3,2,0:T(8,128)(2,1)} %stack.27), calls=%async_computation | async-start | bytes 4194304 | tf_op jit(solution)/shard_map/all_to_all | solution.py:63
  15.8 154.9 %reduce-scatter.5.cloned.1.call-start = ((), (), s32[]{:S(2)}) async-start(), calls=%async_computation.8 | async-start | bytes 655360 | tf_op jit(solution)/shard_map/reduce_scatter | solution.py:72
  64.1 10.9 %copy-start.3 = (s32[12]{0:T(128)S(1)}, s32[12]{0:T(128)}, u32[]{:S(2)}) copy-start(s32[12]{0:T(128)} %param.12) | copy-start | bytes 148
  64.1 47.3 %collective-permute-start.1 = (bf16[8,1,4,256,128]{4,3,0,2,1:T(8,128)(2,1)}, bf16[8,1,4,256,128]{4,3,0,2,1:T(8,128)(2,1)}, u32[]{:S(2)}, u32[]{:S(2)}) collective-permute-start(bf16[8,1,4,256,128]{4,3,0,2,1:T(8,128)(2,1)} %bitcast.5), channel_id=1, source_target_pairs={{4,0},{8,4},{12,8},{16,12},{20,16},{24,20},{28,24},{0,28},{5,1},{9... | collective-permute-start | bytes 6291464 | tf_op jit(solution)/shard_map/ppermute | solution.py:16
  65.3 48.1 %collective-permute-start = (bf16[8,1,4,256,128]{4,3,0,2,1:T(8,128)(2,1)}, bf16[8,1,4,256,128]{4,3,0,2,1:T(8,128)(2,1)}, u32[]{:S(2)}, u32[]{:S(2)}) collective-permute-start(bf16[8,1,4,256,128]{4,3,0,2,1:T(8,128)(2,1)} %bitcast.5), channel_id=1, source_target_pairs={{0,4},{4,8},{8,12},{12,16},{16,20},{20,24},{24,28},{28,0},{1,5},{5... | collective-permute-start | bytes 6291464 | tf_op jit(solution)/shard_map/ppermute | solution.py:13
  75.1 52.0 %copy-start.8 = (pred[12]{0:T(512)(128)(4,1)}, pred[12]{0:T(512)(128)(4,1)S(1)}, u32[]{:S(2)}) copy-start(pred[12]{0:T(512)(128)(4,1)S(1)} %compare_and_fusion) | copy-start | bytes 40
  75.2 52.0 %copy-start.4 = (bf16[8,12]{0,1:T(8,128)(2,1)}, bf16[8,12]{0,1:T(8,128)(2,1)S(1)}, u32[]{:S(2)}) copy-start(bf16[8,12]{0,1:T(8,128)(2,1)S(1)} %compare_convert_fusion) | copy-start | bytes 580
  139.2 31.5 %copy-start.2 = (bf16[4,256,128]{2,1,0:T(8,128)(2,1)S(1)}, bf16[4,256,128]{2,1,0:T(8,128)(2,1)}, u32[]{:S(2)}) copy-start(bf16[4,256,128]{2,1,0:T(8,128)(2,1)} %param.9) | copy-start | bytes 786436
  140.9 9.4 %collective-permute-start.3 = (bf16[4,256,128]{2,0,1:T(4,128)(2,1)S(1)}, bf16[4,256,128]{2,0,1:T(4,128)(2,1)S(1)}, u32[]{:S(2)}, u32[]{:S(2)}) collective-permute-start(bf16[4,256,128]{2,0,1:T(4,128)(2,1)S(1)} %get-tuple-element.13), channel_id=1, source_target_pairs={{28,0},{0,4},{4,8},{8,12},{12,16},{16,20},{20,24},{24,28},{29,1},{... | collective-permute-start | bytes 786440 | tf_op jit(solution)/shard_map/ppermute | solution.py:24
  140.9 9.4 %collective-permute-start.2 = (bf16[4,256,128]{2,0,1:T(4,128)(2,1)S(1)}, bf16[4,256,128]{2,0,1:T(4,128)(2,1)S(1)}, u32[]{:S(2)}, u32[]{:S(2)}) collective-permute-start(bf16[4,256,128]{2,0,1:T(4,128)(2,1)S(1)} %get-tuple-element.12), channel_id=1, source_target_pairs={{4,0},{8,4},{12,8},{16,12},{20,16},{24,20},{28,24},{0,28},{5,1},{9... | collective-permute-start | bytes 786440 | tf_op jit(solution)/shard_map/ppermute | solution.py:24
  151.4 177.7 %reduce-scatter.7.cloned.1.call-start = ((), (), s32[]{:S(2)}) async-start(), calls=%async_computation.9 | async-start | bytes 655360 | tf_op jit(solution)/shard_map/reduce_scatter | solution.py:72
  222.5 45.9 %collective-permute-start.5 = (bf16[8,1,4,256,128]{4,3,0,2,1:T(8,128)(2,1)}, bf16[8,1,4,256,128]{4,3,0,2,1:T(8,128)(2,1)}, u32[]{:S(2)}, u32[]{:S(2)}) collective-permute-start(bf16[8,1,4,256,128]{4,3,0,2,1:T(8,128)(2,1)} %bitcast.20), channel_id=1, source_target_pairs={{4,0},{8,4},{12,8},{16,12},{20,16},{24,20},{28,24},{0,28},{5,1},{9... | collective-permute-start | bytes 6291464 | tf_op jit(solution)/shard_map/ppermute | solution.py:16
  223.0 48.7 %collective-permute-start.4 = (bf16[8,1,4,256,128]{4,3,0,2,1:T(8,128)(2,1)}, bf16[8,1,4,256,128]{4,3,0,2,1:T(8,128)(2,1)}, u32[]{:S(2)}, u32[]{:S(2)}) collective-permute-start(bf16[8,1,4,256,128]{4,3,0,2,1:T(8,128)(2,1)} %bitcast.20), channel_id=1, source_target_pairs={{0,4},{4,8},{8,12},{12,16},{16,20},{20,24},{24,28},{28,0},{1,5},{5... | collective-permute-start | bytes 6291464 | tf_op jit(solution)/shard_map/ppermute | solution.py:13
  278.6 6.9 %copy-start.5 = (bf16[8,12]{0,1:T(8,128)(2,1)S(1)}, bf16[8,12]{0,1:T(8,128)(2,1)}, u32[]{:S(2)}) copy-start(bf16[8,12]{0,1:T(8,128)(2,1)} %copy-done.4) | copy-start | bytes 580
  278.6 6.9 %copy-start.9 = (pred[12]{0:T(512)(128)(4,1)S(1)}, pred[12]{0:T(512)(128)(4,1)}, u32[]{:S(2)}) copy-start(pred[12]{0:T(512)(128)(4,1)} %copy-done.8) | copy-start | bytes 40
  299.2 9.5 %collective-permute-start.7 = (bf16[4,256,128]{2,0,1:T(4,128)(2,1)S(1)}, bf16[4,256,128]{2,0,1:T(4,128)(2,1)S(1)}, u32[]{:S(2)}, u32[]{:S(2)}) collective-permute-start(bf16[4,256,128]{2,0,1:T(4,128)(2,1)S(1)} %get-tuple-element.11), channel_id=1, source_target_pairs={{28,0},{0,4},{4,8},{8,12},{12,16},{16,20},{20,24},{24,28},{29,1},{... | collective-permute-start | bytes 786440 | tf_op jit(solution)/shard_map/ppermute | solution.py:24
  299.3 9.5 %collective-permute-start.6 = (bf16[4,256,128]{2,0,1:T(4,128)(2,1)S(1)}, bf16[4,256,128]{2,0,1:T(4,128)(2,1)S(1)}, u32[]{:S(2)}, u32[]{:S(2)}) collective-permute-start(bf16[4,256,128]{2,0,1:T(4,128)(2,1)S(1)} %get-tuple-element.10), channel_id=1, source_target_pairs={{4,0},{8,4},{12,8},{16,12},{20,16},{24,20},{28,24},{0,28},{5,1},{9... | collective-permute-start | bytes 786440 | tf_op jit(solution)/shard_map/ppermute | solution.py:24
  309.8 177.6 %reduce-scatter.9.cloned.1.call-start = ((), (), s32[]{:S(2)}) async-start(), calls=%async_computation.10 | async-start | bytes 655360 | tf_op jit(solution)/shard_map/reduce_scatter | solution.py:72
  380.9 46.3 %collective-permute-start.9 = (bf16[8,1,4,256,128]{4,3,0,2,1:T(8,128)(2,1)}, bf16[8,1,4,256,128]{4,3,0,2,1:T(8,128)(2,1)}, u32[]{:S(2)}, u32[]{:S(2)}) collective-permute-start(bf16[8,1,4,256,128]{4,3,0,2,1:T(8,128)(2,1)} %bitcast.35), channel_id=1, source_target_pairs={{4,0},{8,4},{12,8},{16,12},{20,16},{24,20},{28,24},{0,28},{5,1},{9... | collective-permute-start | bytes 6291464 | tf_op jit(solution)/shard_map/ppermute | solution.py:16
  381.4 48.7 %collective-permute-start.8 = (bf16[8,1,4,256,128]{4,3,0,2,1:T(8,128)(2,1)}, bf16[8,1,4,256,128]{4,3,0,2,1:T(8,128)(2,1)}, u32[]{:S(2)}, u32[]{:S(2)}) collective-permute-start(bf16[8,1,4,256,128]{4,3,0,2,1:T(8,128)(2,1)} %bitcast.35), channel_id=1, source_target_pairs={{0,4},{4,8},{8,12},{12,16},{16,20},{20,24},{24,28},{28,0},{1,5},{5... | collective-permute-start | bytes 6291464 | tf_op jit(solution)/shard_map/ppermute | solution.py:13
  437.0 6.9 %copy-start.6 = (bf16[8,12]{0,1:T(8,128)(2,1)S(1)}, bf16[8,12]{0,1:T(8,128)(2,1)}, u32[]{:S(2)}) copy-start(bf16[8,12]{0,1:T(8,128)(2,1)} %copy-done.4) | copy-start | bytes 580
  437.0 6.9 %copy-start.10 = (pred[12]{0:T(512)(128)(4,1)S(1)}, pred[12]{0:T(512)(128)(4,1)}, u32[]{:S(2)}) copy-start(pred[12]{0:T(512)(128)(4,1)} %copy-done.8) | copy-start | bytes 40
  457.6 9.5 %collective-permute-start.11 = (bf16[4,256,128]{2,0,1:T(4,128)(2,1)S(1)}, bf16[4,256,128]{2,0,1:T(4,128)(2,1)S(1)}, u32[]{:S(2)}, u32[]{:S(2)}) collective-permute-start(bf16[4,256,128]{2,0,1:T(4,128)(2,1)S(1)} %get-tuple-element.9), channel_id=1, source_target_pairs={{28,0},{0,4},{4,8},{8,12},{12,16},{16,20},{20,24},{24,28},{29,1},{... | collective-permute-start | bytes 786440 | tf_op jit(solution)/shard_map/ppermute | solution.py:24
  457.6 9.4 %collective-permute-start.10 = (bf16[4,256,128]{2,0,1:T(4,128)(2,1)S(1)}, bf16[4,256,128]{2,0,1:T(4,128)(2,1)S(1)}, u32[]{:S(2)}, u32[]{:S(2)}) collective-permute-start(bf16[4,256,128]{2,0,1:T(4,128)(2,1)S(1)} %get-tuple-element.8), channel_id=1, source_target_pairs={{4,0},{8,4},{12,8},{16,12},{20,16},{24,20},{28,24},{0,28},{5,1},{9... | collective-permute-start | bytes 786440 | tf_op jit(solution)/shard_map/ppermute | solution.py:24
  468.2 177.5 %reduce-scatter.11.cloned.1.call-start = ((), (), s32[]{:S(2)}) async-start(), calls=%async_computation.11 | async-start | bytes 655360 | tf_op jit(solution)/shard_map/reduce_scatter | solution.py:72
  539.2 46.2 %collective-permute-start.13 = (bf16[8,1,4,256,128]{4,3,0,2,1:T(8,128)(2,1)}, bf16[8,1,4,256,128]{4,3,0,2,1:T(8,128)(2,1)}, u32[]{:S(2)}, u32[]{:S(2)}) collective-permute-start(bf16[8,1,4,256,128]{4,3,0,2,1:T(8,128)(2,1)} %bitcast.50), channel_id=1, source_target_pairs={{4,0},{8,4},{12,8},{16,12},{20,16},{24,20},{28,24},{0,28},{5,1},{9... | collective-permute-start | bytes 6291464 | tf_op jit(solution)/shard_map/ppermute | solution.py:16
  539.7 48.7 %collective-permute-start.12 = (bf16[8,1,4,256,128]{4,3,0,2,1:T(8,128)(2,1)}, bf16[8,1,4,256,128]{4,3,0,2,1:T(8,128)(2,1)}, u32[]{:S(2)}, u32[]{:S(2)}) collective-permute-start(bf16[8,1,4,256,128]{4,3,0,2,1:T(8,128)(2,1)} %bitcast.50), channel_id=1, source_target_pairs={{0,4},{4,8},{8,12},{12,16},{16,20},{20,24},{24,28},{28,0},{1,5},{5... | collective-permute-start | bytes 6291464 | tf_op jit(solution)/shard_map/ppermute | solution.py:13
  615.9 9.5 %collective-permute-start.15 = (bf16[4,256,128]{2,0,1:T(4,128)(2,1)S(1)}, bf16[4,256,128]{2,0,1:T(4,128)(2,1)S(1)}, u32[]{:S(2)}, u32[]{:S(2)}) collective-permute-start(bf16[4,256,128]{2,0,1:T(4,128)(2,1)S(1)} %get-tuple-element.7), channel_id=1, source_target_pairs={{28,0},{0,4},{4,8},{8,12},{12,16},{16,20},{20,24},{24,28},{29,1},{... | collective-permute-start | bytes 786440 | tf_op jit(solution)/shard_map/ppermute | solution.py:24
  616.0 9.5 %collective-permute-start.14 = (bf16[4,256,128]{2,0,1:T(4,128)(2,1)S(1)}, bf16[4,256,128]{2,0,1:T(4,128)(2,1)S(1)}, u32[]{:S(2)}, u32[]{:S(2)}) collective-permute-start(bf16[4,256,128]{2,0,1:T(4,128)(2,1)S(1)} %get-tuple-element.6), channel_id=1, source_target_pairs={{4,0},{8,4},{12,8},{16,12},{20,16},{24,20},{28,24},{0,28},{5,1},{9... | collective-permute-start | bytes 786440 | tf_op jit(solution)/shard_map/ppermute | solution.py:24
Sparse Core Ops, SparseCore 0:
  151.5 19.1 reduce-scatter.4
  309.9 19.0 reduce-scatter.6
  468.3 19.0 reduce-scatter.8
  626.6 19.0 reduce-scatter.10
